TPU v7x, 256 devices: a whole 4x4x8 slice. The times are simulated.
256 devices in a mesh: seq: 32 (over z_hi, x, core), head: 8 (over y, z_lo).
Axes of the slice: x: 4, y: 4, z: 8 (z_hi: 4, z_lo: 2; z = z_hi * 2 + z_lo), core: 2. Of those that a mesh axis runs over, the one named last changes fastest.
Arguments:
- tokens: bfloat16 [4096, 3072], P('seq', 'head'), may hold values from -5 to 5, as said below
- norm_gains: float32 [5, 3072], replicated, may hold values from 0.25 to 1.75
- window: int32 [24], P('head'), may hold values from 16 to 128, as said below
- self_query: bfloat16 [3072, 3072], P(None, 'head')
- self_key_value: bfloat16 [2, 3072, 1024], P(None, None, 'head')
- self_output: bfloat16 [3072, 3072], P('head'), may hold values from -0.4375 to 0.4375
- shared_key_value: bfloat16 [2, 3072, 1024], P(None, None, 'head')
- cross_query: bfloat16 [3, 3072, 3072], P(None, 'seq', 'head')
- cross_output: bfloat16 [3, 3072, 3072], P(None, 'head', 'seq'), may hold values from -0.4375 to 0.4375
- key_blocks: int32 [3, 32, 16], P(None, 'seq'), may hold values from -1 to 31, as said below
Outputs:
- mixed: float32 [4096, 3072], P('seq', 'head')
Inputs may be any that keep to these rules, and one draw needn't show every extreme that they name: `tokens`: rows may hold near twins of the rows beside them. Some head has a window of exactly 128 and some head one of exactly 16. `key_blocks`: the row of query block b lists distinct blocks at or before b, the first being b itself; it holds min(16, b + 1) blocks and -1 in the remaining slots.
All inputs are finite; a program needn't handle non-finite values.
Results may differ from a plain program's by a relative error of at most 0.04.
Values may be sent and summed in bfloat16 or wider, within the bound.
A program may use at most 64 MiB of HBM per device.

v0:
```python
import jax
import jax.numpy as jnp
from jax import lax
from jax.sharding import PartitionSpec as P

HEAD_WIDTH = 128
KEY_BLOCK_TOKENS = 128
LISTED_BLOCKS = 16
SECTIONS = 3
EPSILON = 1e-06
MASKED = -1e30


def passed_along(value, axis, steps):
    count = lax.axis_size(axis)
    initial, last = (max(0, -steps), min(count, count - steps))
    return lax.ppermute(value, axis, [(source, source + steps) for source in range(initial, last)])


def softmax_rows(scores, allowed):
    scores = jnp.where(allowed, scores, MASKED)
    largest = jnp.max(scores, axis=-1, keepdims=True)
    weights = jnp.exp(scores - largest)
    return (weights / jnp.sum(weights, axis=-1, keepdims=True)).astype(jnp.bfloat16)


def body(
    tokens,
    norm_gains,
    window,
    self_query,
    self_key_value,
    self_output,
    shared_key_value,
    cross_query,
    cross_output,
    key_blocks,
):
    seq_rank = lax.axis_index("seq")
    row_count, local_width = tokens.shape
    kv_columns = self_key_value.shape[2]
    query_columns = self_query.shape[1]
    kv_heads = kv_columns // HEAD_WIDTH
    query_group_width = query_columns // kv_columns
    scale_factor = HEAD_WIDTH ** (-0.5)

    def normed_full(stream, gain_row):
        gathered = lax.all_gather(
            stream.astype(jnp.float32).astype(jnp.bfloat16), "head", axis=1, tiled=True
        ).astype(jnp.float32)
        factor = lax.rsqrt(jnp.mean(gathered * gathered, axis=1, keepdims=True) + EPSILON)
        return (gathered * factor * gain_row[None, :]).astype(jnp.bfloat16)

    def add_branch(stream, partial_value):
        summed = lax.psum_scatter(
            partial_value.astype(jnp.bfloat16), "head", scatter_dimension=1, tiled=True
        ).astype(jnp.float32)
        return stream.astype(jnp.float32) + summed

    def project(inputs, weight):
        return jnp.dot(inputs, weight, preferred_element_type=jnp.float32).astype(jnp.bfloat16)

    first = normed_full(tokens, norm_gains[0])
    query_matrix = project(first, self_query)
    keys_own = project(first, self_key_value[0])
    values_own = project(first, self_key_value[1])
    keys_prev, values_prev = passed_along((keys_own, values_own), "seq", 1)
    near_keys = jnp.concatenate([keys_prev, keys_own], axis=0).reshape(
        2 * row_count, kv_heads, HEAD_WIDTH
    )
    near_values = jnp.concatenate([values_prev, values_own], axis=0).reshape(
        2 * row_count, kv_heads, HEAD_WIDTH
    )
    query_heads = query_matrix.reshape(row_count, kv_heads, query_group_width, HEAD_WIDTH)
    scores = (
        jnp.einsum("tkgd,skd->kgts", query_heads, near_keys, preferred_element_type=jnp.float32)
        * scale_factor
    )
    offsets = (
        jnp.arange(row_count, dtype=jnp.int32)[:, None]
        + row_count
        - jnp.arange(2 * row_count, dtype=jnp.int32)[None, :]
    )
    key_pos = seq_rank * row_count - row_count + jnp.arange(2 * row_count, dtype=jnp.int32)
    window_bounds = window.reshape(kv_heads, query_group_width)
    allowed = (
        (offsets >= 0)[None, None]
        & (offsets[None, None] < window_bounds[:, :, None, None])
        & (key_pos >= 0)[None, None, None, :]
    )
    probs = softmax_rows(scores, allowed)
    context = jnp.einsum("kgts,skd->tkgd", probs, near_values, preferred_element_type=jnp.float32)
    context = context.astype(jnp.bfloat16).reshape(row_count, query_columns)
    stream = add_branch(tokens, jnp.dot(context, self_output, preferred_element_type=jnp.float32))
    cache_in = normed_full(stream, norm_gains[1])
    cached_key_rows = project(cache_in, shared_key_value[0])
    cached_value_rows = project(cache_in, shared_key_value[1])
    all_keys, all_values = (
        lax.all_gather(cached_key_rows, "seq", axis=0, tiled=True),
        lax.all_gather(cached_value_rows, "seq", axis=0, tiled=True),
    )
    key_lookup_matrix = all_keys.reshape(-1, KEY_BLOCK_TOKENS, kv_columns)
    value_lookup_matrix = all_values.reshape(-1, KEY_BLOCK_TOKENS, kv_columns)
    query_blocks = row_count // KEY_BLOCK_TOKENS
    inner = jnp.arange(KEY_BLOCK_TOKENS, dtype=jnp.int32)
    block_ids = seq_rank * query_blocks + jnp.arange(query_blocks, dtype=jnp.int32)
    query_pos = block_ids[:, None] * KEY_BLOCK_TOKENS + inner[None, :]
    for section in range(SECTIONS):
        section_in = normed_full(stream, norm_gains[2 + section])
        query_matrix = jnp.dot(
            section_in,
            lax.all_gather(cross_query[section], "seq", axis=0, tiled=True),
            preferred_element_type=jnp.float32,
        ).astype(jnp.bfloat16)
        lists = key_blocks[section]
        clamped_index = jnp.maximum(lists, 0)
        picked_keys = jnp.take(key_lookup_matrix, clamped_index.reshape(-1), axis=0).reshape(
            query_blocks, LISTED_BLOCKS * KEY_BLOCK_TOKENS, kv_heads, HEAD_WIDTH
        )
        picked_values = jnp.take(value_lookup_matrix, clamped_index.reshape(-1), axis=0).reshape(
            query_blocks, LISTED_BLOCKS * KEY_BLOCK_TOKENS, kv_heads, HEAD_WIDTH
        )
        query_heads = query_matrix.reshape(
            query_blocks, KEY_BLOCK_TOKENS, kv_heads, query_group_width, HEAD_WIDTH
        )
        scores = (
            jnp.einsum(
                "btkgd,bskd->bkgts", query_heads, picked_keys, preferred_element_type=jnp.float32
            )
            * scale_factor
        )
        listed_pos = (clamped_index[:, :, None] * KEY_BLOCK_TOKENS + inner[None, None, :]).reshape(
            query_blocks, LISTED_BLOCKS * KEY_BLOCK_TOKENS
        )
        present = jnp.repeat(lists >= 0, KEY_BLOCK_TOKENS, axis=1)
        allowed = present[:, None, :] & (listed_pos[:, None, :] <= query_pos[:, :, None])
        probs = softmax_rows(scores, allowed[:, None, None])
        context = jnp.einsum(
            "bkgts,bskd->btkgd", probs, picked_values, preferred_element_type=jnp.float32
        )
        context = context.astype(jnp.bfloat16).reshape(row_count, query_columns)
        partial_value = jnp.dot(
            context,
            lax.all_gather(cross_output[section], "seq", axis=1, tiled=True),
            preferred_element_type=jnp.float32,
        )
        stream = add_branch(stream, partial_value)
    return stream


def solution(mesh):
    placed = (
        P("seq", "head"),
        P(),
        P("head"),
        P(None, "head"),
        P(None, None, "head"),
        P("head", None),
        P(None, None, "head"),
        P(None, "seq", "head"),
        P(None, "head", "seq"),
        P(None, "seq", None),
    )
    return jax.shard_map(
        body, mesh=mesh, in_specs=placed, out_specs=P("seq", "head"), check_vma=False
    )
```

profile of v0, /device:TPU:2, one launch (start us, length us, event | category | flops | bytes accessed | tf_op | source)
XLA Modules:
  0.0 703.6 jit_solution(482095804169605450)
XLA Ops:
  6.5 1.9 fusion.87
  8.4 32.0 %all_gather.37 = bf16[128,3072]{1,0:T(8,128)(2,1)S(1)} all-gather(bf16[128,384]{1,0:T(8,128)(2,1)} %param.12), channel_id=1, replica_groups=mesh['seq'=32,'head'=8] {'head'}, dimensions={1}, use_global_device_ids=true | all-gather | bytes 884736 | tf_op jit(solution)/shard_map/all_gather | solution.py:48
  40.7 1.7 convolution_convert_fusion.8
  42.5 1.9 collective-permute-start.1
  44.8 3.5 collective-permute-start
  50.9 1.2 copy.68
  52.2 46.3 %reduce-scatter.13.cloned.1.call-done = bf16[384,128]{1,0:T(8,128)(2,1)} async-done(((bf16[3072,128]{1,0:T(8,128)(2,1)}), bf16[384,128]{1,0:T(8,128)(2,1)}) %reduce-scatter.13.cloned.1.call-update) | async-done | bytes 98320
  99.5 30.8 %all_gather.38 = bf16[128,3072]{1,0:T(8,128)(2,1)S(1)} all-gather(bf16[128,384]{1,0:T(8,128)(2,1)S(1)} %fusion.73), channel_id=1, replica_groups=mesh['seq'=32,'head'=8] {'head'}, dimensions={1}, use_global_device_ids=true | all-gather | bytes 884736 | tf_op jit(solution)/shard_map/all_gather | solution.py:48
  130.6 2.2 convolution_convert_fusion.7
  132.9 2.2 convolution_convert_fusion.6
  135.1 1.6 fusion.86
  136.8 1.7 fusion.85
  139.1 4.1 compare_and_fusion
  143.1 39.4 %all-gather.15.cloned.1.call-done = bf16[4096,128]{1,0:T(8,128)(2,1)} async-done(((bf16[128,128]{1,0:T(8,128)(2,1)}), bf16[4096,128]{1,0:T(8,128)(2,1)}) %all-gather.15.cloned.1.call-update) | async-done | bytes 1048592 | tf_op jit(solution)/shard_map/all_gather | solution.py:100
  182.5 2.7 gather_fusion
  185.2 49.4 %all-gather.17.cloned.1.call-done = bf16[4096,128]{1,0:T(8,128)(2,1)} async-done(((bf16[128,128]{1,0:T(8,128)(2,1)}), bf16[4096,128]{1,0:T(8,128)(2,1)}) %all-gather.17.cloned.1.call-update) | async-done | bytes 1048592 | tf_op jit(solution)/shard_map/all_gather | solution.py:99
  234.6 2.7 gather_fusion.1
  237.3 2.4 broadcast_select_fusion.4
  239.7 49.5 %all-gather.19.cloned.1.call-done = bf16[1,3072,384]{2,1,0:T(8,128)(2,1)} async-done(((bf16[1,96,384]{2,1,0:T(8,128)(2,1)}), bf16[1,3072,384]{2,1,0:T(8,128)(2,1)}) %all-gather.19.cloned.1.call-update) | async-done | bytes 2359312 | tf_op jit(solution)/shard_map/all_gather | solution.py:112
  289.2 2.3 fusion.43
  291.6 1.8 fusion.89
  295.2 48.1 %all-gather.21.cloned.1.call-done = bf16[1,384,3072]{1,2,0:T(8,128)(2,1)} async-done(((bf16[1,384,96]{1,2,0:T(8,128)(2,1)}), bf16[1,384,3072]{1,2,0:T(8,128)(2,1)}) %all-gather.21.cloned.1.call-update) | async-done | bytes 2359312 | tf_op jit(solution)/shard_map/all_gather | solution.py:144
  343.4 2.6 convolution_convert_fusion.2
  345.9 1.2 copy.70
  348.7 1.9 gather_fusion.4
  350.6 2.7 gather_fusion.5
  353.3 2.7 gather_fusion.2
  356.0 2.7 gather_fusion.3
  358.6 3.0 broadcast_select_fusion
  361.6 26.7 %reduce-scatter.15.cloned.1.call-done = bf16[384,128]{1,0:T(8,128)(2,1)} async-done(((bf16[3072,128]{1,0:T(8,128)(2,1)}), bf16[384,128]{1,0:T(8,128)(2,1)}) %reduce-scatter.15.cloned.1.call-update) | async-done | bytes 98320
  389.3 31.5 %all_gather.43 = bf16[128,3072]{1,0:T(8,128)(2,1)S(1)} all-gather(bf16[128,384]{1,0:T(8,128)(2,1)S(1)} %fusion.79), channel_id=1, replica_groups=mesh['seq'=32,'head'=8] {'head'}, dimensions={1}, use_global_device_ids=true | all-gather | bytes 884736 | tf_op jit(solution)/shard_map/all_gather | solution.py:48
  421.1 21.4 %all-gather.23.cloned.1.call-done = bf16[1,3072,384]{2,1,0:T(8,128)(2,1)} async-done(((bf16[1,96,384]{2,1,0:T(8,128)(2,1)}), bf16[1,3072,384]{2,1,0:T(8,128)(2,1)}) %all-gather.23.cloned.1.call-update) | async-done | bytes 2359312 | tf_op jit(solution)/shard_map/all_gather | solution.py:112
  442.5 2.3 fusion.46
  444.9 1.8 fusion.90
  448.5 48.3 %all-gather.25.cloned.1.call-done = bf16[1,384,3072]{1,2,0:T(8,128)(2,1)} async-done(((bf16[1,384,96]{1,2,0:T(8,128)(2,1)}), bf16[1,384,3072]{1,2,0:T(8,128)(2,1)}) %all-gather.25.cloned.1.call-update) | async-done | bytes 2359312 | tf_op jit(solution)/shard_map/all_gather | solution.py:144
  496.8 2.5 convolution_convert_fusion.1
  499.4 1.1 copy.72
  501.9 39.7 %reduce-scatter.17.cloned.1.call-done = bf16[384,128]{1,0:T(8,128)(2,1)} async-done(((bf16[3072,128]{1,0:T(8,128)(2,1)}), bf16[384,128]{1,0:T(8,128)(2,1)}) %reduce-scatter.17.cloned.1.call-update) | async-done | bytes 98320
  542.7 31.2 %all_gather.46 = bf16[128,3072]{1,0:T(8,128)(2,1)S(1)} all-gather(bf16[128,384]{1,0:T(8,128)(2,1)S(1)} %fusion.74), channel_id=1, replica_groups=mesh['seq'=32,'head'=8] {'head'}, dimensions={1}, use_global_device_ids=true | all-gather | bytes 884736 | tf_op jit(solution)/shard_map/all_gather | solution.py:48
  574.2 21.6 %all-gather.27.cloned.1.call-done = bf16[1,3072,384]{2,1,0:T(8,128)(2,1)} async-done(((bf16[1,96,384]{2,1,0:T(8,128)(2,1)}), bf16[1,3072,384]{2,1,0:T(8,128)(2,1)}) %all-gather.27.cloned.1.call-update) | async-done | bytes 2359312 | tf_op jit(solution)/shard_map/all_gather | solution.py:112
  595.8 2.9 fusion.49
  598.7 1.0 copy.52
  599.7 1.8 fusion.91
  602.6 1.4 fusion.40
  604.0 46.1 %all-gather.29.cloned.1.call-done = bf16[1,384,3072]{1,2,0:T(8,128)(2,1)} async-done(((bf16[1,384,96]{1,2,0:T(8,128)(2,1)}), bf16[1,384,3072]{1,2,0:T(8,128)(2,1)}) %all-gather.29.cloned.1.call-update) | async-done | bytes 2359312 | tf_op jit(solution)/shard_map/all_gather | solution.py:144
  650.1 2.6 convolution_convert_fusion
  652.7 1.2 copy.74
  653.9 41.1 %reduce-scatter.19.cloned.1.call-done = bf16[384,128]{1,0:T(8,128)(2,1)} async-done(((bf16[3072,128]{1,0:T(8,128)(2,1)}), bf16[384,128]{1,0:T(8,128)(2,1)}) %reduce-scatter.19.cloned.1.call-update) | async-done | bytes 98320
  (92 shorter events, 17.3 us)
Async XLA Ops:
  6.5 43.8 %copy-start = (bf16[384,3072]{1,0:T(8,128)(2,1)S(1)}, bf16[384,3072]{1,0:T(8,128)(2,1)}, u32[]{:S(2)}) copy-start(bf16[384,3072]{1,0:T(8,128)(2,1)} %param.17) | copy-start | bytes 7077892
  6.5 91.9 %reduce-scatter.13.cloned.1.call-start = ((), (), s32[]{:S(2)}) async-start(), calls=%async_computation.12 | async-start | bytes 884736
  6.5 37.8 %copy-start.7 = (bf16[2,3072,128]{2,1,0:T(8,128)(2,1)S(1)}, bf16[2,3072,128]{2,1,0:T(8,128)(2,1)}, u32[]{:S(2)}) copy-start(bf16[2,3072,128]{2,1,0:T(8,128)(2,1)} %param.16) | copy-start | bytes 4718596
  40.7 7.7 %copy-start.6 = (bf16[3072,384]{1,0:T(8,128)(2,1)S(1)}, bf16[3072,384]{1,0:T(8,128)(2,1)}, u32[]{:S(2)}) copy-start(bf16[3072,384]{1,0:T(8,128)(2,1)} %param.15) | copy-start | bytes 7077892
  42.5 6.8 collective-permute-start.1
  44.8 4.4 copy-start.8
  44.8 5.2 collective-permute-start
  50.3 49.2 %copy-start.1 = (bf16[128,384]{1,0:T(8,128)(2,1)S(1)}, bf16[128,384]{1,0:T(8,128)(2,1)}, u32[]{:S(2)}) copy-start(bf16[128,384]{1,0:T(8,128)(2,1)} %param.12) | copy-start | bytes 294916
  52.1 130.4 %all-gather.15.cloned.1.call-start = ((), (), s32[]{:S(2)}) async-start(), calls=%async_computation.4 | async-start | bytes 1081344 | tf_op jit(solution)/shard_map/all_gather | solution.py:100
  132.8 5.8 copy-start.5
  132.8 101.8 %all-gather.17.cloned.1.call-start = ((), (), s32[]{:S(2)}) async-start(), calls=%async_computation.5 | async-start | bytes 1081344 | tf_op jit(solution)/shard_map/all_gather | solution.py:99
  135.1 154.1 %all-gather.19.cloned.1.call-start = ((), (), s32[]{:S(2)}) async-start(), calls=%async_computation.6 | async-start | bytes 2433024 | tf_op jit(solution)/shard_map/all_gather | solution.py:112
  136.8 206.6 %all-gather.21.cloned.1.call-start = ((), (), s32[]{:S(2)}) async-start(), calls=%async_computation.7 | async-start | bytes 2433024 | tf_op jit(solution)/shard_map/all_gather | solution.py:144
  138.5 249.8 %reduce-scatter.15.cloned.1.call-start = ((), (), s32[]{:S(2)}) async-start(), calls=%async_computation.13 | async-start | bytes 884736
  293.4 1.0 copy-start.4
  347.2 95.3 %all-gather.23.cloned.1.call-start = ((), (), s32[]{:S(2)}) async-start(), calls=%async_computation.8 | async-start | bytes 2433024 | tf_op jit(solution)/shard_map/all_gather | solution.py:112
  347.9 148.9 %all-gather.25.cloned.1.call-start = ((), (), s32[]{:S(2)}) async-start(), calls=%async_computation.9 | async-start | bytes 2433024 | tf_op jit(solution)/shard_map/all_gather | solution.py:144
  348.7 193.0 %reduce-scatter.17.cloned.1.call-start = ((), (), s32[]{:S(2)}) async-start(), calls=%async_computation.14 | async-start | bytes 884736
  446.7 1.0 copy-start.3
  500.5 95.2 %all-gather.27.cloned.1.call-start = ((), (), s32[]{:S(2)}) async-start(), calls=%async_computation.10 | async-start | bytes 2433024 | tf_op jit(solution)/shard_map/all_gather | solution.py:112
  501.1 149.0 %all-gather.29.cloned.1.call-start = ((), (), s32[]{:S(2)}) async-start(), calls=%async_computation.11 | async-start | bytes 2433024 | tf_op jit(solution)/shard_map/all_gather | solution.py:144
  501.9 193.2 %reduce-scatter.19.cloned.1.call-start = ((), (), s32[]{:S(2)}) async-start(), calls=%async_computation.15 | async-start | bytes 884736
  601.5 1.0 copy-start.2
Sparse Core Ops, SparseCore 0:
  52.2 46.1 reduce-scatter.12
  132.9 49.5 all-gather.14
  185.1 49.4 all-gather.16
  237.0 52.1 all-gather.18
  291.6 51.7 all-gather.20
  347.3 40.9 reduce-scatter.14
  390.8 51.5 all-gather.22
  445.0 51.7 all-gather.24
  500.6 40.9 reduce-scatter.16
  544.0 51.7 all-gather.26
  598.3 51.7 all-gather.28
  654.0 40.9 reduce-scatter.18
where the time goes:
time: 705 us; the launch traced here: 704 us
  waiting for transfers between devices  481 us (68%)
  blocking collectives  126 us (18%)
  local copies, waits for them, and re-layouts  32.8 us (5%)
  matrix products  31.8 us (5%)
  between operations  14 us (2%)
  other arithmetic  12.8 us (2%)
    unnamed x16, waiting for transfers between devices  157 us
    all_gather x3, waiting for transfers between devices, body(): lax.all_gather(cross_output[section], 'seq', axis=1, tiled=True)  143 us
    all_gather x4, blocking collectives, normed_full(): lax.all_gather(stream.astype(jnp.float32).astype(jnp.bfloat16), 'head', a...  126 us
    all_gather x3, waiting for transfers between devices, body(): lax.all_gather(cross_query[section], 'seq', axis=0, tiled=True)  92.5 us
    all_gather x1, waiting for transfers between devices, body(): lax.all_gather(cached_key_rows, 'seq', axis=0, tiled=True)  49.4 us
    all_gather x1, waiting for transfers between devices, body(): lax.all_gather(cached_value_rows, 'seq', axis=0, tiled=True)  39.4 us
  transfers between devices with their start and end apart: 14, of which 13 were waited for; matrix products, arithmetic and copies ran while one was open for 8% of the time, Pallas kernels for 0%

commit v1 on v0

--- a/solution.py
+++ b/solution.py
@@ -141,7 +141,12 @@
         context = context.astype(jnp.bfloat16).reshape(row_count, query_columns)
         partial_value = jnp.dot(
             context,
-            lax.all_gather(cross_output[section], "seq", axis=1, tiled=True),
+            jnp.concatenate(
+                lax.all_to_all(
+                    jnp.stack([cross_output[section]] * lax.axis_size("seq")), "seq", 0, 0
+                ),
+                axis=1,
+            ),
             preferred_element_type=jnp.float32,
         )
         stream = add_branch(stream, partial_value)

time: 705 us -> 647 us (0.918)
  waiting for transfers between devices: 481 us -> 372 us
  starting transfers between devices: 5.86 us -> 30.7 us
  blocking collectives: 126 us -> 143 us
    all_gather x3 -> x0, waiting for transfers between devices: 143 us -> none  [body(): lax.all_gather(cross_output[section], 'seq', axis=1, tiled=True)]
    unnamed x16 -> x13, waiting for transfers between devices: 157 us -> 184 us
    all_to_all x0 -> x3, starting transfers between devices: none -> 24.9 us  [body(): lax.all_to_all(jnp.stack([cross_output[section]] * lax.axis_size('seq')),...]
    all_gather x1, waiting for transfers between devices: 39.4 us -> 58 us  [body(): lax.all_gather(cached_value_rows, 'seq', axis=0, tiled=True)]
    all_gather x4, blocking collectives: 126 us -> 143 us  [normed_full(): lax.all_gather(stream.astype(jnp.float32).astype(jnp.bfloat16), 'head', a...]
    all_gather x3, waiting for transfers between devices: 92.5 us -> 78 us  [body(): lax.all_gather(cross_query[section], 'seq', axis=0, tiled=True)]
  transfers between devices with their start and end apart: 14 -> 14, of which waited for: 13 -> 10; matrix products, arithmetic and copies ran while one was open for 8% -> 10% of each run, Pallas kernels for 0% -> 0%
where the time goes in v1:
time: 647 us; the launch traced here: 646 us
  waiting for transfers between devices  372 us (57%)
  blocking collectives  143 us (22%)
  local copies, waits for them, and re-layouts  38 us (6%)
  matrix products  34.5 us (5%)
  starting transfers between devices  30.7 us (5%)
  between operations  13.7 us (2%)
  other arithmetic  13.3 us (2%)
    unnamed x13, waiting for transfers between devices  184 us
    all_gather x4, blocking collectives, normed_full(): lax.all_gather(stream.astype(jnp.float32).astype(jnp.bfloat16), 'head', a...  143 us
    all_gather x3, waiting for transfers between devices, body(): lax.all_gather(cross_query[section], 'seq', axis=0, tiled=True)  78 us
    all_gather x1, waiting for transfers between devices, body(): lax.all_gather(cached_value_rows, 'seq', axis=0, tiled=True)  58 us
    all_gather x1, waiting for transfers between devices, body(): lax.all_gather(cached_key_rows, 'seq', axis=0, tiled=True)  52 us
    all_to_all x3, starting transfers between devices, body(): lax.all_to_all(jnp.stack([cross_output[section]] * lax.axis_size('seq')),...  24.9 us
  transfers between devices with their start and end apart: 14, of which 10 were waited for; matrix products, arithmetic and copies ran while one was open for 10% of the time, Pallas kernels for 0%

profile of v1, /device:TPU:2, one launch (start us, length us, event | category | flops | bytes accessed | tf_op | source)
XLA Modules:
  0.0 645.6 jit_solution(13086367070947031729)
XLA Ops:
  6.5 1.3 fusion.83
  7.8 32.2 %all_gather.28 = bf16[128,3072]{1,0:T(8,128)(2,1)S(1)} all-gather(bf16[128,384]{1,0:T(8,128)(2,1)} %param.12), channel_id=1, replica_groups=mesh['seq'=32,'head'=8] {'head'}, dimensions={1}, use_global_device_ids=true | all-gather | bytes 884736 | tf_op jit(solution)/shard_map/all_gather | solution.py:48
  40.3 1.7 convolution_convert_fusion.8
  42.0 1.9 collective-permute-start.1
  44.4 3.5 collective-permute-start
  51.7 46.3 %reduce-scatter.13.cloned.1.call-done = bf16[384,128]{1,0:T(8,128)(2,1)} async-done(((bf16[3072,128]{1,0:T(8,128)(2,1)}), bf16[384,128]{1,0:T(8,128)(2,1)}) %reduce-scatter.13.cloned.1.call-update) | async-done | bytes 98320
  99.0 30.8 %all_gather.29 = bf16[128,3072]{1,0:T(8,128)(2,1)S(1)} all-gather(bf16[128,384]{1,0:T(8,128)(2,1)S(1)} %fusion.70), channel_id=1, replica_groups=mesh['seq'=32,'head'=8] {'head'}, dimensions={1}, use_global_device_ids=true | all-gather | bytes 884736 | tf_op jit(solution)/shard_map/all_gather | solution.py:48
  130.1 2.2 convolution_convert_fusion.7
  132.4 2.2 convolution_convert_fusion.6
  134.7 1.6 fusion.82
  137.3 1.6 stack.9
  138.9 10.1 %all-to-all-start = ((bf16[32,384,96]{1,2,0:T(8,128)(2,1)}), bf16[32,384,96]{1,2,0:T(8,128)(2,1)}, u32[]{:S(2)}, u32[]{:S(2)}) async-start(bf16[32,384,96]{1,2,0:T(8,128)(2,1)} %stack.9), calls=%async_computation | async-start | bytes 4718592 | tf_op jit(solution)/shard_map/all_to_all | solution.py:145
  150.2 4.1 compare_and_fusion
  154.2 58.0 %all-gather.9.cloned.1.call-done = bf16[4096,128]{1,0:T(8,128)(2,1)} async-done(((bf16[128,128]{1,0:T(8,128)(2,1)}), bf16[4096,128]{1,0:T(8,128)(2,1)}) %all-gather.9.cloned.1.call-update) | async-done | bytes 1048592 | tf_op jit(solution)/shard_map/all_gather | solution.py:100
  212.2 2.7 gather_fusion
  214.9 52.0 %all-gather.11.cloned.1.call-done = bf16[4096,128]{1,0:T(8,128)(2,1)} async-done(((bf16[128,128]{1,0:T(8,128)(2,1)}), bf16[4096,128]{1,0:T(8,128)(2,1)}) %all-gather.11.cloned.1.call-update) | async-done | bytes 1048592 | tf_op jit(solution)/shard_map/all_gather | solution.py:99
  266.8 2.6 gather_fusion.1
  269.5 2.3 broadcast_select_fusion.4
  271.8 49.6 %all-gather.13.cloned.1.call-done = bf16[1,3072,384]{2,1,0:T(8,128)(2,1)} async-done(((bf16[1,96,384]{2,1,0:T(8,128)(2,1)}), bf16[1,3072,384]{2,1,0:T(8,128)(2,1)}) %all-gather.13.cloned.1.call-update) | async-done | bytes 2359312 | tf_op jit(solution)/shard_map/all_gather | solution.py:112
  321.4 2.9 fusion.40
  325.4 1.8 fusion.85
  328.2 1.4 fusion.31
  329.6 2.6 convolution_convert_fusion.2
  334.1 1.6 stack.10
  335.7 7.4 %all-to-all-start.1 = ((bf16[32,384,96]{1,2,0:T(8,128)(2,1)}), bf16[32,384,96]{1,2,0:T(8,128)(2,1)}, u32[]{:S(2)}, u32[]{:S(2)}) async-start(bf16[32,384,96]{1,2,0:T(8,128)(2,1)} %stack.10), calls=%async_computation.1 | async-start | bytes 4718592 | tf_op jit(solution)/shard_map/all_to_all | solution.py:145
  343.2 1.9 gather_fusion.4
  345.1 2.6 gather_fusion.5
  347.7 2.6 gather_fusion.2
  350.4 2.6 gather_fusion.3
  353.0 2.9 broadcast_select_fusion
  355.9 41.3 %reduce-scatter.15.cloned.1.call-done = bf16[384,128]{1,0:T(8,128)(2,1)} async-done(((bf16[3072,128]{1,0:T(8,128)(2,1)}), bf16[384,128]{1,0:T(8,128)(2,1)}) %reduce-scatter.15.cloned.1.call-update) | async-done | bytes 98320
  398.3 40.4 %all_gather.33 = bf16[128,3072]{1,0:T(8,128)(2,1)S(1)} all-gather(bf16[128,384]{1,0:T(8,128)(2,1)S(1)} %fusion.76), channel_id=1, replica_groups=mesh['seq'=32,'head'=8] {'head'}, dimensions={1}, use_global_device_ids=true | all-gather | bytes 884736 | tf_op jit(solution)/shard_map/all_gather | solution.py:48
  439.0 14.3 %all-gather.15.cloned.1.call-done = bf16[1,3072,384]{2,1,0:T(8,128)(2,1)} async-done(((bf16[1,96,384]{2,1,0:T(8,128)(2,1)}), bf16[1,3072,384]{2,1,0:T(8,128)(2,1)}) %all-gather.15.cloned.1.call-update) | async-done | bytes 2359312 | tf_op jit(solution)/shard_map/all_gather | solution.py:112
  453.3 2.9 fusion.43
  457.2 1.8 fusion.86
  460.1 1.4 fusion.34
  461.5 2.6 convolution_convert_fusion.1
  464.1 1.2 copy.75
  466.1 1.6 stack.11
  467.7 7.4 %all-to-all-start.2 = ((bf16[32,384,96]{1,2,0:T(8,128)(2,1)}), bf16[32,384,96]{1,2,0:T(8,128)(2,1)}, u32[]{:S(2)}, u32[]{:S(2)}) async-start(bf16[32,384,96]{1,2,0:T(8,128)(2,1)} %stack.11), calls=%async_computation.2 | async-start | bytes 4718592 | tf_op jit(solution)/shard_map/all_to_all | solution.py:145
  475.2 53.8 %reduce-scatter.17.cloned.1.call-done = bf16[384,128]{1,0:T(8,128)(2,1)} async-done(((bf16[3072,128]{1,0:T(8,128)(2,1)}), bf16[384,128]{1,0:T(8,128)(2,1)}) %reduce-scatter.17.cloned.1.call-update) | async-done | bytes 98320
  530.1 40.1 %all_gather.35 = bf16[128,3072]{1,0:T(8,128)(2,1)S(1)} all-gather(bf16[128,384]{1,0:T(8,128)(2,1)S(1)} %fusion.71), channel_id=1, replica_groups=mesh['seq'=32,'head'=8] {'head'}, dimensions={1}, use_global_device_ids=true | all-gather | bytes 884736 | tf_op jit(solution)/shard_map/all_gather | solution.py:48
  570.4 14.1 %all-gather.17.cloned.1.call-done = bf16[1,3072,384]{2,1,0:T(8,128)(2,1)} async-done(((bf16[1,96,384]{2,1,0:T(8,128)(2,1)}), bf16[1,3072,384]{2,1,0:T(8,128)(2,1)}) %all-gather.17.cloned.1.call-update) | async-done | bytes 2359312 | tf_op jit(solution)/shard_map/all_gather | solution.py:112
  584.5 2.9 fusion.46
  588.5 1.8 fusion.87
  591.3 1.4 fusion.37
  592.7 2.6 convolution_convert_fusion
  596.5 40.8 %reduce-scatter.19.cloned.1.call-done = bf16[384,128]{1,0:T(8,128)(2,1)} async-done(((bf16[3072,128]{1,0:T(8,128)(2,1)}), bf16[384,128]{1,0:T(8,128)(2,1)}) %reduce-scatter.19.cloned.1.call-update) | async-done | bytes 98320
  (104 shorter events, 22.2 us)
Async XLA Ops:
  6.5 43.3 %copy-start = (bf16[384,3072]{1,0:T(8,128)(2,1)S(1)}, bf16[384,3072]{1,0:T(8,128)(2,1)}, u32[]{:S(2)}) copy-start(bf16[384,3072]{1,0:T(8,128)(2,1)} %param.17) | copy-start | bytes 7077892
  6.5 91.4 %reduce-scatter.13.cloned.1.call-start = ((), (), s32[]{:S(2)}) async-start(), calls=%async_computation.12 | async-start | bytes 884736
  6.5 37.4 %copy-start.11 = (bf16[2,3072,128]{2,1,0:T(8,128)(2,1)S(1)}, bf16[2,3072,128]{2,1,0:T(8,128)(2,1)}, u32[]{:S(2)}) copy-start(bf16[2,3072,128]{2,1,0:T(8,128)(2,1)} %param.16) | copy-start | bytes 4718596
  40.3 7.7 %copy-start.10 = (bf16[3072,384]{1,0:T(8,128)(2,1)S(1)}, bf16[3072,384]{1,0:T(8,128)(2,1)}, u32[]{:S(2)}) copy-start(bf16[3072,384]{1,0:T(8,128)(2,1)} %param.15) | copy-start | bytes 7077892
  42.0 6.8 %collective-permute-start.1 = (bf16[128,128]{1,0:T(8,128)(2,1)S(1)}, bf16[128,128]{1,0:T(8,128)(2,1)S(1)}, u32[]{:S(2)}, u32[]{:S(2)}) collective-permute-start(bf16[128,128]{1,0:T(8,128)(2,1)S(1)} %convolution_convert_fusion.8), channel_id=1, source_target_pairs={{0,8},{8,16},{16,24},{24,32},{32,40},{40,48},{48,56},{56,64},{64,7... | collective-permute-start | bytes 98312 | tf_op jit(solution)/shard_map/ppermute | solution.py:17
  44.4 4.4 copy-start.12
  44.4 5.2 collective-permute-start
  49.9 49.1 %copy-start.1 = (bf16[128,384]{1,0:T(8,128)(2,1)S(1)}, bf16[128,384]{1,0:T(8,128)(2,1)}, u32[]{:S(2)}) copy-start(bf16[128,384]{1,0:T(8,128)(2,1)} %param.12) | copy-start | bytes 294916
  51.7 160.6 %all-gather.9.cloned.1.call-start = ((), (), s32[]{:S(2)}) async-start(), calls=%async_computation.7 | async-start | bytes 1081344 | tf_op jit(solution)/shard_map/all_gather | solution.py:100
  130.1 4.5 copy-start.13
  132.3 134.5 %all-gather.11.cloned.1.call-start = ((), (), s32[]{:S(2)}) async-start(), calls=%async_computation.8 | async-start | bytes 1081344 | tf_op jit(solution)/shard_map/all_gather | solution.py:99
  134.6 186.8 %all-gather.13.cloned.1.call-start = ((), (), s32[]{:S(2)}) async-start(), calls=%async_computation.9 | async-start | bytes 2433024 | tf_op jit(solution)/shard_map/all_gather | solution.py:112
  138.9 10.2 %copy-start.5 = (s32[3,1,16]{2,1,0:T(1,128)S(1)}, s32[3,1,16]{2,1,0:T(1,128)}, u32[]{:S(2)}) copy-start(s32[3,1,16]{2,1,0:T(1,128)} %param.21) | copy-start | bytes 580
  138.9 190.7 %all-to-all-start = ((bf16[32,384,96]{1,2,0:T(8,128)(2,1)}), bf16[32,384,96]{1,2,0:T(8,128)(2,1)}, u32[]{:S(2)}, u32[]{:S(2)}) async-start(bf16[32,384,96]{1,2,0:T(8,128)(2,1)} %stack.9), calls=%async_computation | async-start | bytes 4718592 | tf_op jit(solution)/shard_map/all_to_all | solution.py:145
  149.0 248.2 %reduce-scatter.15.cloned.1.call-start = ((), (), s32[]{:S(2)}) async-start(), calls=%async_computation.13 | async-start | bytes 884736
  154.2 167.2 %copy-start.14 = (f32[128]{0:T(128)S(1)}, f32[128]{0:T(128)}, u32[]{:S(2)}) copy-start(f32[128]{0:T(128)} %copy-done.13) | copy-start | bytes 1540
  327.2 1.0 copy-start.4
  333.5 119.8 %all-gather.15.cloned.1.call-start = ((), (), s32[]{:S(2)}) async-start(), calls=%async_computation.10 | async-start | bytes 2433024 | tf_op jit(solution)/shard_map/all_gather | solution.py:112
  335.7 7.5 %copy-start.9 = (s32[16]{0:T(128)S(1)}, s32[16]{0:T(128)}, u32[]{:S(2)}) copy-start(s32[16]{0:T(128)} %get-tuple-element.32) | copy-start | bytes 196
  335.7 7.5 %copy-start.8 = (s32[16]{0:T(128)S(1)}, s32[16]{0:T(128)}, u32[]{:S(2)}) copy-start(s32[16]{0:T(128)} %get-tuple-element.30) | copy-start | bytes 196
  335.7 125.8 %all-to-all-start.1 = ((bf16[32,384,96]{1,2,0:T(8,128)(2,1)}), bf16[32,384,96]{1,2,0:T(8,128)(2,1)}, u32[]{:S(2)}, u32[]{:S(2)}) async-start(bf16[32,384,96]{1,2,0:T(8,128)(2,1)} %stack.10), calls=%async_computation.1 | async-start | bytes 4718592 | tf_op jit(solution)/shard_map/all_to_all | solution.py:145
  343.1 9.9 %copy-start.6 = (pred[16]{0:T(512)(128)(4,1)S(1)}, pred[16]{0:T(512)(128)(4,1)}, u32[]{:S(2)}) copy-start(pred[16]{0:T(512)(128)(4,1)} %get-tuple-element.29) | copy-start | bytes 52
  343.1 9.9 %copy-start.7 = (pred[16]{0:T(512)(128)(4,1)S(1)}, pred[16]{0:T(512)(128)(4,1)}, u32[]{:S(2)}) copy-start(pred[16]{0:T(512)(128)(4,1)} %get-tuple-element.31) | copy-start | bytes 52
  343.1 185.9 %reduce-scatter.17.cloned.1.call-start = ((), (), s32[]{:S(2)}) async-start(), calls=%async_computation.14 | async-start | bytes 884736
  459.0 1.0 copy-start.3
  465.3 119.2 %all-gather.17.cloned.1.call-start = ((), (), s32[]{:S(2)}) async-start(), calls=%async_computation.11 | async-start | bytes 2433024 | tf_op jit(solution)/shard_map/all_gather | solution.py:112
  467.7 125.0 %all-to-all-start.2 = ((bf16[32,384,96]{1,2,0:T(8,128)(2,1)}), bf16[32,384,96]{1,2,0:T(8,128)(2,1)}, u32[]{:S(2)}, u32[]{:S(2)}) async-start(bf16[32,384,96]{1,2,0:T(8,128)(2,1)} %stack.11), calls=%async_computation.2 | async-start | bytes 4718592 | tf_op jit(solution)/shard_map/all_to_all | solution.py:145
  475.1 162.2 %reduce-scatter.19.cloned.1.call-start = ((), (), s32[]{:S(2)}) async-start(), calls=%async_computation.15 | async-start | bytes 884736
  590.3 1.0 copy-start.2
Sparse Core Ops, SparseCore 0:
  51.8 46.1 reduce-scatter.12
  132.5 79.7 all-gather.8
  214.8 51.9 all-gather.10
  269.2 52.1 all-gather.12
  333.6 63.6 reduce-scatter.14
  399.7 53.5 all-gather.14
  465.4 63.5 reduce-scatter.16
  531.6 52.9 all-gather.16
  596.7 40.6 reduce-scatter.18
